TPU v7x, 32 devices: a whole 2x2x4 slice. The times are simulated.
32 devices in a mesh: slab: 8 (over y, x, core), coil: 4 (over z).
Axes of the slice: x: 2, y: 2, z: 4, core: 2. Of those that a mesh axis runs over, the one named last changes fastest.
Arguments:
- sensitivity: float32 [4, 2, 16, 256, 128], P('coil', None, 'slab'), may hold values from -4 to 4
- kspace: float32 [4, 2, 16, 256, 128], P('coil', None, 'slab')
- sampling: int32 [16, 256, 128], P('slab'), may hold values 0 or 1
- prior_image: float32 [2, 16, 256, 128], P(None, 'slab', 'coil')
- w_first: bfloat16 [32, 2, 3, 3, 3], replicated, may hold values from -0.875 to 0.875
- w_middle: bfloat16 [3, 32, 32, 3, 3, 3], replicated, may hold values from -0.21875 to 0.21875
- w_last: bfloat16 [2, 32, 3, 3, 3], replicated, may hold values from -0.21875 to 0.21875
Outputs:
- solution: float32 [2, 16, 256, 128], P(None, 'slab', 'coil')
- refined: float32 [2, 16, 256, 128], P(None, 'slab', 'coil')
Inputs may be any that keep to these rules, and one draw needn't show every extreme that they name: sampling marks the measured ky-kz positions of each readout plane.
All inputs are finite; a program needn't handle non-finite values. No bound on the sum of `sampling` on one device may be relied on, other than what follows from the above.
Results may differ from a plain program's by a relative error of at most 0.0015.
Values may be sent and summed in bfloat16 or wider, within the bound.
A program may use at most 128 MiB of HBM per device.

v0:
```python
import functools

import jax
import jax.numpy as jnp
import numpy as np
from jax import lax
from jax.experimental import pallas as pl
from jax.experimental.pallas import tpu as pltpu
from jax.sharding import PartitionSpec as P

LAMBDA = 0.5
MESH = pl.DeviceIdType.MESH


def dft_parts(length):
    positions = np.arange(length)
    angles = 2.0 * np.pi / length * (positions[:, None] * positions[None, :] % length)
    return np.cos(angles) / np.sqrt(length), np.sin(angles) / np.sqrt(length)


def halves(table):
    table = table.astype(np.float32)
    high = table.astype(jnp.bfloat16)
    low = (table - high.astype(np.float32)).astype(jnp.bfloat16)
    return jnp.asarray(high), jnp.asarray(low)


def split(values):
    high = values.astype(jnp.bfloat16)
    return high, (values - high.astype(jnp.float32)).astype(jnp.bfloat16)


def multiply(left, right):
    return jnp.dot(left, right, preferred_element_type=jnp.float32)


def transform(real, imag, y_high, y_low, z_high, z_low):
    planes = len(real)
    rows, width = real[0].shape
    field = jnp.concatenate([jnp.concatenate(real, axis=1), jnp.concatenate(imag, axis=1)], axis=0)
    high, low = split(field)
    both = multiply(y_high[...], jnp.concatenate([high, low], axis=1))
    span = planes * width
    field = both[:, :span] + both[:, span:] + multiply(y_low[...], high)
    field = jnp.concatenate(
        [
            jnp.concatenate([field[:rows, p * width : (p + 1) * width], field[rows:, p * width : (p + 1) * width]], axis=1)
            for p in range(planes)
        ],
        axis=0,
    )
    high, low = split(field)
    both = multiply(jnp.concatenate([high, low], axis=0), z_high[...])
    span = planes * rows
    field = both[:span] + both[span:] + multiply(high, z_low[...])
    pieces = [field[p * rows : (p + 1) * rows] for p in range(planes)]
    return [piece[:, :width] for piece in pieces], [piece[:, width:] for piece in pieces]


def total_of(values):
    return jnp.sum(jnp.sum(values, axis=0, keepdims=True), axis=1, keepdims=True)


def gradients_kernel(
    shares, coils, maps, measured, mask, prior, y_high, y_low, z_high, z_low,
    out, part, arrived, rhs, spectrum, own_residual, residual, note, notes,
    block_send, block_recv, note_send, note_recv,
):
    slab = lax.axis_index("slab")
    coil = lax.axis_index("coil")
    devices = shares * coils
    me = slab * coils + coil
    planes = maps.shape[1]
    block = prior.shape[2]
    tables = (y_high, y_low, z_high, z_low)

    def device_at(distance):
        other = lax.rem(me + distance, devices)
        return (other // coils, lax.rem(other, coils))

    barrier = pltpu.get_barrier_semaphore()
    for distance in range(1, devices):
        pl.semaphore_signal(barrier, inc=1, device_id=device_at(distance), device_id_type=MESH)
    pl.semaphore_wait(barrier, devices - 1)

    def rows_of(index):
        return pl.ds(pl.multiple_of(index * block, block), block)

    mine = rows_of(coil)

    def scatter(phase):
        copies = []
        for distance in range(1, coils):
            target = lax.rem(coil + distance, coils)
            copies.append(
                pltpu.make_async_remote_copy(
                    src_ref=part.at[phase, :, :, rows_of(target)],
                    dst_ref=arrived.at[phase, distance - 1],
                    send_sem=block_send.at[2 * phase, distance - 1],
                    recv_sem=block_recv.at[2 * phase, distance - 1],
                    device_id=(slab, target),
                    device_id_type=MESH,
                )
            )
        for copy in copies:
            copy.start()
        return copies

    def gather(buffer, phase):
        copies = []
        for distance in range(1, coils):
            copies.append(
                pltpu.make_async_remote_copy(
                    src_ref=buffer.at[:, :, mine],
                    dst_ref=buffer.at[:, :, mine],
                    send_sem=block_send.at[2 * phase + 1, distance - 1],
                    recv_sem=block_recv.at[2 * phase + 1, distance - 1],
                    device_id=(slab, lax.rem(coil + distance, coils)),
                    device_id_type=MESH,
                )
            )
        for copy in copies:
            copy.start()
        return copies

    def tell(phase):
        copies = []
        for distance in range(1, devices):
            copies.append(
                pltpu.make_async_remote_copy(
                    src_ref=note.at[phase],
                    dst_ref=notes.at[phase, distance - 1],
                    send_sem=note_send.at[phase, distance - 1],
                    recv_sem=note_recv.at[phase, distance - 1],
                    device_id=device_at(distance),
                    device_id_type=MESH,
                )
            )
        for copy in copies:
            copy.start()
        return copies

    def finish(copies):
        for copy in copies:
            copy.wait()

    lanes = lax.broadcasted_iota(jnp.int32, (1, note.shape[2]), 1)

    def write_note(phase, values):
        line = jnp.zeros(lanes.shape, jnp.float32)
        for index, value in enumerate(values):
            line = jnp.where(lanes == index, value, line)
        note[phase] = line

    def read_notes(phase, count):
        line = note[phase]
        for distance in range(1, devices):
            line = line + notes[phase, distance - 1]
        return [jnp.sum(jnp.where(lanes == index, line, 0.0), axis=1, keepdims=True) for index in range(count)]

    def backward_part(real, imag, phase):
        imag, real = transform(imag, real, *tables)
        for p in range(planes):
            part[phase, 0, p] = maps[0, p] * real[p] + maps[1, p] * imag[p]
            part[phase, 1, p] = maps[0, p] * imag[p] - maps[1, p] * real[p]

    def forward(image):
        real = [maps[0, p] * image(0, p) - maps[1, p] * image(1, p) for p in range(planes)]
        imag = [maps[0, p] * image(1, p) + maps[1, p] * image(0, p) for p in range(planes)]
        real, imag = transform(real, imag, *tables)
        sampled = [mask[p].astype(jnp.float32) for p in range(planes)]
        return [[real[p] * sampled[p] for p in range(planes)], [imag[p] * sampled[p] for p in range(planes)]]

    def reduced(phase, h, p):
        value = part[phase, h, p, mine]
        for distance in range(1, coils):
            value = value + arrived[phase, distance - 1, h, p]
        return value

    sampled = [mask[p].astype(jnp.float32) for p in range(planes)]
    backward_part(
        [measured[0, p] * sampled[p] for p in range(planes)], [measured[1, p] * sampled[p] for p in range(planes)], 0
    )
    finish(scatter(0))
    entries = [(h, p) for h in range(2) for p in range(planes)]
    for h, p in entries:
        rhs[h, p, mine] = reduced(0, h, p) + LAMBDA * prior[h, p]
    finish(gather(rhs, 0))

    norm = jnp.zeros((1, 1), jnp.float32)
    for h, p in entries:
        value = rhs[h, p, mine]
        norm = norm + total_of(value * value)
    result = forward(lambda h, p: rhs[h, p])
    energy = LAMBDA * norm
    for h, p in entries:
        spectrum[h, p] = result[h][p]
        energy = energy + total_of(result[h][p] * result[h][p])
    write_note(0, [norm, energy])
    first_notes = tell(0)
    backward_part([spectrum[0, p] for p in range(planes)], [spectrum[1, p] for p in range(planes)], 1)
    second_parts = scatter(1)
    finish(first_notes)
    norm, curvature = read_notes(0, 2)
    step = norm / curvature
    finish(second_parts)
    norm_next = jnp.zeros((1, 1), jnp.float32)
    cross = jnp.zeros((1, 1), jnp.float32)
    for h, p in entries:
        direction = rhs[h, p, mine]
        value = direction - step * (reduced(1, h, p) + LAMBDA * direction)
        own_residual[h, p] = value
        residual[h, p, mine] = value.astype(jnp.bfloat16)
        norm_next = norm_next + total_of(value * value)
        cross = cross + LAMBDA * total_of(value * direction)
    finish(gather(residual, 1))
    result = forward(lambda h, p: residual[h, p].astype(jnp.float32))
    energy = LAMBDA * norm_next
    for h, p in entries:
        energy = energy + total_of(result[h][p] * result[h][p])
        cross = cross + total_of(result[h][p] * spectrum[h, p])
    write_note(1, [norm_next, energy, cross])
    finish(tell(1))
    norm_next, energy, cross = read_notes(1, 3)
    ratio = norm_next / norm
    curvature = energy + 2.0 * ratio * cross + ratio * ratio * curvature
    step_next = norm_next / curvature
    for h, p in entries:
        direction = rhs[h, p, mine]
        out[h, p] = step * direction + step_next * (own_residual[h, p] + ratio * direction)


def gradients(maps, measured, mask, prior):
    planes, rows, width = mask.shape
    block = prior.shape[2]
    shares = lax.axis_size("slab")
    coils = lax.axis_size("coil")
    cosine, sine = dft_parts(rows)
    y_tables = halves(np.block([[cosine, sine], [-sine, cosine]]))
    cosine, sine = dft_parts(width)
    z_tables = halves(np.block([[cosine, -sine], [sine, cosine]]))
    image = (2, planes, rows, width)
    brick = (2, planes, block, width)
    return pl.pallas_call(
        functools.partial(gradients_kernel, shares, coils),
        out_shape=jax.ShapeDtypeStruct(brick, jnp.float32),
        in_specs=[pl.BlockSpec(memory_space=pltpu.VMEM)] * 8,
        out_specs=pl.BlockSpec(memory_space=pltpu.VMEM),
        scratch_shapes=[
            pltpu.VMEM((2,) + image, jnp.float32),
            pltpu.VMEM((2, coils - 1) + brick, jnp.float32),
            pltpu.VMEM(image, jnp.float32),
            pltpu.VMEM(image, jnp.float32),
            pltpu.VMEM(brick, jnp.float32),
            pltpu.VMEM(image, jnp.bfloat16),
            pltpu.VMEM((2, 1, 128), jnp.float32),
            pltpu.VMEM((2, shares * coils - 1, 1, 128), jnp.float32),
            pltpu.SemaphoreType.DMA((4, coils - 1)),
            pltpu.SemaphoreType.DMA((4, coils - 1)),
            pltpu.SemaphoreType.DMA((2, shares * coils - 1)),
            pltpu.SemaphoreType.DMA((2, shares * coils - 1)),
        ],
        compiler_params=pltpu.CompilerParams(
            collective_id=0, has_side_effects=True, vmem_limit_bytes=56 * 1024 * 1024
        ),
    )(maps, measured, mask, prior, *y_tables, *z_tables)


def row_halo(cells, width):
    count = lax.axis_size("coil")
    tail = cells[:, :, cells.shape[2] - width :]
    head = cells[:, :, :width]
    return jnp.concatenate(
        [
            lax.ppermute(tail, "coil", [(i, i + 1) for i in range(count - 1)]),
            cells,
            lax.ppermute(head, "coil", [(i + 1, i) for i in range(count - 1)]),
        ],
        axis=2,
    )


def block_weights(weight, x_outs, y_outs, in_pad, out_pad):
    weight = jnp.pad(weight, ((0, out_pad), (0, in_pad), (0, 0), (0, 0), (0, 0)))
    weight = jnp.transpose(weight, (4, 0, 3, 2, 1))
    parts = []
    for x_out in range(x_outs):
        for y_out in range(y_outs):
            spread = ((0, 0), (0, 0), (y_out, y_outs - 1 - y_out), (x_out, x_outs - 1 - x_out), (0, 0))
            parts.append(jnp.pad(weight, spread))
    stacked = jnp.stack(parts)
    return stacked.reshape(stacked.shape[0] * stacked.shape[1] * stacked.shape[2], -1)


def conv_rows(weight_ref, source, sink, rows, planes, x_outs, y_outs, group, top, height, last):
    width = source.shape[-1]
    channels = source.shape[2]
    weight_rows = weight_ref.shape[0]
    outs = weight_rows // (3 * x_outs * y_outs)
    lanes = lax.broadcasted_iota(jnp.int32, (outs, width), 1)
    depth = (y_outs + 2) * (x_outs + 2) * channels

    def step(index, carry):
        y = index * y_outs
        for first in range(0, planes, x_outs * group):
            blocks = [
                source[pl.ds(y, y_outs + 2), first + k * x_outs : first + (k + 1) * x_outs + 2].reshape(depth, width)
                for k in range(group)
            ]
            taken = jnp.concatenate(blocks, axis=1) if group > 1 else blocks[0]
            product = jnp.dot(weight_ref[...], taken, preferred_element_type=jnp.float32)
            for x_out in range(x_outs):
                for y_out in range(y_outs):
                    base = (x_out * y_outs + y_out) * 3 * outs
                    y_now = y + y_out
                    inside = jnp.logical_and(top + y_now >= 0, top + y_now < height)
                    for k in range(group):
                        span = slice(k * width, (k + 1) * width)
                        before = product[base : base + outs, span]
                        centre = product[base + outs : base + 2 * outs, span]
                        after = product[base + 2 * outs : base + 3 * outs, span]
                        before = jnp.where(lanes == 0, 0.0, pltpu.roll(before, 1, 1))
                        after = jnp.where(lanes == width - 1, 0.0, pltpu.roll(after, width - 1, 1))
                        value = centre + before + after
                        plane = first + k * x_outs + x_out
                        if last:
                            sink[y_now, plane] = value
                        else:
                            value = jnp.where(inside, jnp.maximum(value, 0.0), 0.0)
                            sink[y_now, plane + 1] = value.astype(jnp.bfloat16)
        return carry

    lax.fori_loop(0, rows // y_outs, step, 0)


def denoise_kernel(x_outs, y_outs, group, rows, block_rows, height, features, first, middle, final, out, even, odd):
    planes = features.shape[1] - 2
    layers = middle.shape[0] + 2
    top = lax.axis_index("coil") * block_rows + lax.axis_index("slab") * rows
    buffers = (even, odd)
    for buffer in buffers:
        edge = jnp.zeros((buffer.shape[0],) + buffer.shape[2:], buffer.dtype)
        buffer[:, 0] = edge
        buffer[:, planes + 1] = edge
    shared = (planes, x_outs, y_outs, group)
    left = layers - 1
    conv_rows(first, features, even, rows + 2 * left, *shared, top - left, height, False)
    for layer in range(layers - 2):
        left = left - 1
        conv_rows(
            middle.at[layer], buffers[layer % 2], buffers[(layer + 1) % 2],
            rows + 2 * left, *shared, top - left, height, False,
        )
    conv_rows(final, buffers[(layers - 2) % 2], out, rows, *shared, top, height, True)


def denoise(features, w_first, w_middle, w_last, rows, block_rows, height):
    planes = features.shape[1]
    width = features.shape[3]
    channels = w_first.shape[0]
    layers = w_middle.shape[0] + 2
    x_outs = 2 if planes % 2 == 0 else 1
    y_outs = 2 if rows % 2 == 0 else 1
    group = 2 if (planes // x_outs) % 2 == 0 else 1
    in_rows = 16
    features = jnp.pad(features, ((0, 0), (1, 1), (0, in_rows - features.shape[2]), (0, 0)))
    first = block_weights(w_first, x_outs, y_outs, in_rows - w_first.shape[1], 0)
    middle = jnp.stack([block_weights(w_middle[m], x_outs, y_outs, 0, 0) for m in range(layers - 2)])
    final = block_weights(w_last, x_outs, y_outs, 0, -w_last.shape[0] % 8)
    outs = w_last.shape[0]
    held = (rows + 2 * (layers - 1), planes + 2, channels, width)
    result = pl.pallas_call(
        functools.partial(denoise_kernel, x_outs, y_outs, group, rows, block_rows, height),
        out_shape=jax.ShapeDtypeStruct((rows, planes, outs + -outs % 8, width), jnp.float32),
        in_specs=[pl.BlockSpec(memory_space=pltpu.VMEM)] * 4,
        out_specs=pl.BlockSpec(memory_space=pltpu.VMEM),
        scratch_shapes=[pltpu.VMEM(held, jnp.bfloat16), pltpu.VMEM(held, jnp.bfloat16)],
        compiler_params=pltpu.CompilerParams(vmem_limit_bytes=48 * 1024 * 1024),
    )(features, first, middle, final)
    return result[:, :, :outs]


def body(sensitivity, kspace, sampling, prior_image, w_first, w_middle, w_last):
    brick = gradients(sensitivity[0], kspace[0], sampling, prior_image)
    len_y = sampling.shape[1]
    block_rows = prior_image.shape[2]
    halo = w_middle.shape[0] + 2
    shares = lax.axis_size("slab")
    rows = block_rows // shares
    mine = row_halo(brick.astype(jnp.bfloat16), halo)
    mine = jnp.transpose(mine, (2, 1, 0, 3))
    pieces = jnp.stack([mine[s * rows : (s + 1) * rows + 2 * halo] for s in range(shares)])
    taken = lax.all_to_all(pieces, "slab", 0, 0)
    features = jnp.moveaxis(taken, 0, 1).reshape((rows + 2 * halo, -1) + taken.shape[3:])
    correction = denoise(features, w_first, w_middle, w_last, rows, block_rows, len_y)
    local = prior_image.shape[1]
    pieces = jnp.moveaxis(correction.reshape((rows, shares, local) + correction.shape[2:]), 1, 0)
    taken = lax.all_to_all(pieces, "slab", 0, 0)
    correction = jnp.transpose(taken.reshape((block_rows,) + taken.shape[2:]), (2, 1, 0, 3))
    return (brick, brick + correction)


def solution(mesh):
    placed = (
        P("coil", None, "slab", None, None),
        P("coil", None, "slab", None, None),
        P("slab", None, None),
        P(None, "slab", "coil", None),
        P(),
        P(),
        P(),
    )
    return jax.shard_map(
        body,
        mesh=mesh,
        in_specs=placed,
        out_specs=(P(None, "slab", "coil", None), P(None, "slab", "coil", None)),
        check_vma=False,
    )
```

profile of v0, /device:TPU:0, one launch (start us, length us, event | category | flops | bytes accessed | tf_op | source)
XLA Modules:
  0.0 131.7 jit_solution(12838465178049375550)
XLA Ops:
  0.6 0.0 copy-start.4
  0.6 65.3 %shard_map.122 = f32[2,2,64,128]{3,2,1,0:T(8,128)} custom-call(f32[2,2,256,128]{3,2,1,0:T(8,128)} %bitcast.108, f32[2,2,256,128]{3,2,1,0:T(8,128)} %bitcast.109, s32[2,256,128]{2,1,0:T(8,128)} %mask.1, f32[2,2,64,128]{3,2,1,0:T(8,128)} %prior.1, bf16[512,512]{1,0:T(8,128)(2,1)} %constant.11.clone.y_high, bf16[512,512]{1,0:T(8,128)(2,1)} %constant.12.clone.y_low, ...), custom_call_target="tpu_custom_call" | custom-call | tf_op jit(solution)/shard_map/pallas_call | solution.py:244
  66.0 0.9 convert_element_type.41
  66.9 0.0 copy-start.5
  66.9 0.0 copy-start.7
  66.9 0.6 fusion.8
  67.5 2.5 %collective-permute-start = (bf16[2,2,5,128]{3,2,1,0:T(8,128)(2,1)}, bf16[2,2,5,128]{3,2,1,0:T(8,128)(2,1)S(1)}, u32[]{:S(2)}, u32[]{:S(2)}) collective-permute-start(bf16[2,2,5,128]{3,2,1,0:T(8,128)(2,1)} %get-tuple-element.21), channel_id=1, source_target_pairs={{0,1},{1,2},{2,3},{4,5},{5,6},{6,7},{8,9},{9,10},{10,11},{12,13},{... | collective-permute-start | bytes 15368 | tf_op jit(solution)/shard_map/ppermute | solution.py:275
  70.0 0.0 copy-done.5
  70.0 1.3 collective-permute-start.1
  71.4 0.0 copy-start.8
  71.4 0.3 pad_bitcast_fusion.11
  71.7 0.1 pad_bitcast_fusion.15
  71.8 0.3 copy-done.8
  72.1 0.1 pad_bitcast_fusion.20
  72.2 0.6 pad_bitcast_fusion.3
  72.8 0.4 pad_maximum_fusion.1
  73.2 0.4 pad_maximum_fusion.2
  73.6 0.4 pad_maximum_fusion
  74.0 1.1 pad_maximum_fusion.4
  75.1 0.1 pad_maximum_fusion.5
  75.2 2.4 %copy.32 = bf16[4,3,32,4,4,32]{5,4,3,2,1,0:T(4,128)(2,1)} copy(bf16[4,3,32,4,4,32]{5,2,1,3,4,0:T(8,128)(2,1)S(1)} %pad_maximum_fusion.1) | data formatting | bytes 786432 | tf_op jit(solution)/shard_map/stack | solution.py:291
  77.6 4.6 %stack_reshape.10 = bf16[1,384,512]{2,1,0:T(8,128)(2,1)} reshape(bf16[4,3,32,4,4,32]{5,4,3,2,1,0:T(4,128)(2,1)} %copy.32) | data formatting | bytes 786432 | tf_op jit(solution)/shard_map/stack;reshape | solution.py:368
  82.2 2.4 %copy.33 = bf16[4,3,32,4,4,32]{5,4,3,2,1,0:T(4,128)(2,1)} copy(bf16[4,3,32,4,4,32]{5,2,1,3,4,0:T(8,128)(2,1)S(1)} %pad_maximum_fusion.2) | data formatting | bytes 786432 | tf_op jit(solution)/shard_map/stack | solution.py:291
  84.6 4.6 %stack_reshape.11 = bf16[1,384,512]{2,1,0:T(8,128)(2,1)} reshape(bf16[4,3,32,4,4,32]{5,4,3,2,1,0:T(4,128)(2,1)} %copy.33) | data formatting | bytes 786432 | tf_op jit(solution)/shard_map/stack;reshape | solution.py:368
  89.1 1.2 copy.31
  90.3 0.0 copy-start
  90.4 1.5 %stack_reshape.9 = bf16[1,384,512]{2,1,0:T(8,128)(2,1)S(1)} reshape(bf16[4,3,32,4,4,32]{5,4,3,2,1,0:T(4,128)(2,1)S(1)} %copy.31) | data formatting | bytes 786432 | tf_op jit(solution)/shard_map/stack;reshape | solution.py:368
  91.9 0.5 copy.30
  92.4 0.0 copy-start.6
  92.4 0.7 reshape.20
  93.1 0.1 copy.35.first
  93.3 0.2 copy.34
  93.5 0.3 reshape.21.final
  93.8 0.0 collective-permute-done
  93.8 0.0 collective-permute-done.1
  94.0 0.8 copy.28
  94.8 3.6 %all-to-all-start = ((bf16[8,18,2,2,128]{4,3,2,1,0:T(2,128)(2,1)}), bf16[8,18,2,2,128]{4,3,2,1,0:T(2,128)(2,1)S(1)}, u32[]{:S(2)}, u32[]{:S(2)}) async-start(bf16[8,18,2,2,128]{4,3,2,1,0:T(2,128)(2,1)} %copy.28), calls=%async_computation | async-start | bytes 294912 | tf_op jit(solution)/shard_map/all_to_all | solution.py:393
  98.4 0.0 copy-done.2
  98.4 0.0 copy-done.3
  98.4 0.1 pad_maximum_fusion.3.middle
  98.5 5.5 %all-to-all-done = bf16[8,18,2,2,128]{4,3,2,1,0:T(2,128)(2,1)S(1)} async-done(((bf16[8,18,2,2,128]{4,3,2,1,0:T(2,128)(2,1)}), bf16[8,18,2,2,128]{4,3,2,1,0:T(2,128)(2,1)S(1)}, u32[]{:S(2)}, u32[]{:S(2)}) %all-to-all-start) | async-done | bytes 147488 | tf_op jit(solution)/shard_map/all_to_all | solution.py:393
  104.0 0.1 copy.29
  104.1 0.2 pad.84.features
  104.4 0.0 copy-start.1
  104.4 18.0 %shard_map.123 = f32[8,16,8,128]{3,2,1,0:T(8,128)S(1)} custom-call(bf16[18,18,16,128]{3,2,1,0:T(8,128)(2,1)S(1)} %pad.84.features, bf16[384,256]{1,0:T(8,128)(2,1)S(1)} %copy.35.first, bf16[3,384,512]{2,1,0:T(8,128)(2,1)S(1)} %pad_maximum_fusion.3.middle, bf16[96,512]{1,0:T(8,128)(2,1)S(1)} %reshape.21.final), custom_call_target="tpu_custom_call" | custom-call | tf_op jit(solution)/shard_map/pallas_call | solution.py:372
  122.5 7.9 %all_to_all.10 = f32[8,8,2,2,128]{4,3,2,1,0:T(2,128)S(1)} all-to-all(f32[8,8,2,2,128]{4,3,2,1,0:T(2,128)S(1)} %bitcast.107), channel_id=1, replica_groups=mesh['slab'=8,'coil'=4] {'slab'}, dimensions={0} | all-to-all | bytes 262144 | tf_op jit(solution)/shard_map/all_to_all | solution.py:398
  130.4 0.7 bitcast_add_fusion
  131.0 0.7 copy.49
  (21 shorter events, 0.3 us)
Async XLA Ops:
  0.6 70.7 %copy-start.4 = (bf16[3,32,32,3,3,3]{2,1,5,4,3,0:T(8,128)(2,1)S(1)}, bf16[3,32,32,3,3,3]{2,1,5,4,3,0:T(8,128)(2,1)}, u32[]{:S(2)}) copy-start(bf16[3,32,32,3,3,3]{2,1,5,4,3,0:T(8,128)(2,1)} %param.16) | copy-start | bytes 497668
  66.9 3.1 %copy-start.5 = (bf16[2,2,64,128]{3,2,1,0:T(8,128)(2,1)}, bf16[2,2,64,128]{3,2,1,0:T(8,128)(2,1)S(1)}, u32[]{:S(2)}) copy-start(bf16[2,2,64,128]{3,2,1,0:T(8,128)(2,1)S(1)} %convert_element_type.41) | copy-start | bytes 196612
  66.9 4.8 %copy-start.7 = (bf16[32,2,3,3,3]{0,1,4,3,2:T(2,128)(2,1)S(1)}, bf16[32,2,3,3,3]{0,1,4,3,2:T(2,128)(2,1)}, u32[]{:S(2)}) copy-start(bf16[32,2,3,3,3]{0,1,4,3,2:T(2,128)(2,1)} %param.15) | copy-start | bytes 10372
  67.5 26.3 %collective-permute-start = (bf16[2,2,5,128]{3,2,1,0:T(8,128)(2,1)}, bf16[2,2,5,128]{3,2,1,0:T(8,128)(2,1)S(1)}, u32[]{:S(2)}, u32[]{:S(2)}) collective-permute-start(bf16[2,2,5,128]{3,2,1,0:T(8,128)(2,1)} %get-tuple-element.21), channel_id=1, source_target_pairs={{0,1},{1,2},{2,3},{4,5},{5,6},{6,7},{8,9},{9,10},{10,11},{12,13},{... | collective-permute-start | bytes 15368 | tf_op jit(solution)/shard_map/ppermute | solution.py:275
  70.0 23.8 %collective-permute-start.1 = (bf16[2,2,5,128]{3,2,1,0:T(8,128)(2,1)}, bf16[2,2,5,128]{3,2,1,0:T(8,128)(2,1)S(1)}, u32[]{:S(2)}, u32[]{:S(2)}) collective-permute-start(bf16[2,2,5,128]{3,2,1,0:T(8,128)(2,1)} %get-tuple-element.22), channel_id=1, source_target_pairs={{1,0},{2,1},{3,2},{5,4},{6,5},{7,6},{9,8},{10,9},{11,10},{13,12},{... | collective-permute-start | bytes 15368 | tf_op jit(solution)/shard_map/ppermute | solution.py:277
  71.4 0.7 copy-start.8
  90.3 1.5 %copy-start = (bf16[4,3,32,4,4,16]{2,5,1,3,4,0:T(8,128)(2,1)S(1)}, bf16[4,3,32,4,4,16]{2,5,1,3,4,0:T(8,128)(2,1)}, u32[]{:S(2)}) copy-start(bf16[4,3,32,4,4,16]{2,5,1,3,4,0:T(8,128)(2,1)} %pad_maximum_fusion.4) | copy-start | bytes 589828
  92.4 1.4 %copy-start.6 = (bf16[2,2,64,128]{3,2,1,0:T(8,128)(2,1)S(1)}, bf16[2,2,64,128]{3,2,1,0:T(8,128)(2,1)}, u32[]{:S(2)}) copy-start(bf16[2,2,64,128]{3,2,1,0:T(8,128)(2,1)} %copy-done.5) | copy-start | bytes 196612
  93.1 5.3 %copy-start.2 = (bf16[1,384,512]{2,1,0:T(8,128)(2,1)S(1)}, bf16[1,384,512]{2,1,0:T(8,128)(2,1)}, u32[]{:S(2)}) copy-start(bf16[1,384,512]{2,1,0:T(8,128)(2,1)} %stack_reshape.10) | copy-start | bytes 1179652
  93.1 5.3 %copy-start.3 = (bf16[1,384,512]{2,1,0:T(8,128)(2,1)S(1)}, bf16[1,384,512]{2,1,0:T(8,128)(2,1)}, u32[]{:S(2)}) copy-start(bf16[1,384,512]{2,1,0:T(8,128)(2,1)} %stack_reshape.11) | copy-start | bytes 1179652
  94.8 9.3 %all-to-all-start = ((bf16[8,18,2,2,128]{4,3,2,1,0:T(2,128)(2,1)}), bf16[8,18,2,2,128]{4,3,2,1,0:T(2,128)(2,1)S(1)}, u32[]{:S(2)}, u32[]{:S(2)}) async-start(bf16[8,18,2,2,128]{4,3,2,1,0:T(2,128)(2,1)} %copy.28), calls=%async_computation | async-start | bytes 294912 | tf_op jit(solution)/shard_map/all_to_all | solution.py:393
  104.4 26.0 %copy-start.1 = (f32[2,2,64,128]{3,2,1,0:T(8,128)S(1)}, f32[2,2,64,128]{3,2,1,0:T(8,128)}, u32[]{:S(2)}) copy-start(f32[2,2,64,128]{3,2,1,0:T(8,128)} %shard_map.122) | copy-start | bytes 393220
where the time goes:
time: 132 us
  Pallas kernels  83.4 us (63%)
  local copies, waits for them, and re-layouts  22.4 us (17%)
  blocking collectives  7.89 us (6%)
  starting transfers between devices  7.35 us (6%)
  waiting for transfers between devices  5.52 us (4%)
  other arithmetic  4.18 us (3%)
    pallas_call x1, Pallas kernels, gradients(): pl.pallas_call(functools.partial(gradients_kernel, shares, coils), out_sh...  65.3 us
    pallas_call x1, Pallas kernels, denoise(): pl.pallas_call(functools.partial(denoise_kernel, x_outs, y_outs, group, r...  18 us
    another operation x3, local copies, waits for them, and re-layouts, denoise(): jnp.stack([block_weights(w_middle[m], x_outs, y_outs, 0, 0) for m in rang...  10.6 us
    all_to_all x1, blocking collectives, body(): taken = lax.all_to_all(pieces, 'slab', 0, 0)  7.89 us
    another operation x9, local copies, waits for them, and re-layouts, block_weights(): stacked = jnp.stack(parts)  7.72 us
    all_to_all x1, waiting for transfers between devices, body(): taken = lax.all_to_all(pieces, 'slab', 0, 0)  5.51 us
    all_to_all x1, starting transfers between devices, body(): taken = lax.all_to_all(pieces, 'slab', 0, 0)  3.6 us
  transfers between devices with their start and end apart: 3, of which 1 were waited for; matrix products, arithmetic and copies ran while one was open for 17% of the time, Pallas kernels for 0%

commit v1 on v0

--- a/solution.py
+++ b/solution.py
@@ -35,26 +35,17 @@
 
 
 def transform(real, imag, y_high, y_low, z_high, z_low):
-    planes = len(real)
-    rows, width = real[0].shape
-    field = jnp.concatenate([jnp.concatenate(real, axis=1), jnp.concatenate(imag, axis=1)], axis=0)
-    high, low = split(field)
+    rows, width = real.shape
+    high, low = split(jnp.concatenate([real, imag], axis=1))
     both = multiply(y_high[...], jnp.concatenate([high, low], axis=1))
-    span = planes * width
-    field = both[:, :span] + both[:, span:] + multiply(y_low[...], high)
+    field = both[:, : 2 * width] + both[:, 2 * width :] + multiply(y_low[...], high)
     field = jnp.concatenate(
-        [
-            jnp.concatenate([field[:rows, p * width : (p + 1) * width], field[rows:, p * width : (p + 1) * width]], axis=1)
-            for p in range(planes)
-        ],
-        axis=0,
+        [field[:rows, :width] + field[rows:, width:], field[:rows, width:] - field[rows:, :width]], axis=1
     )
     high, low = split(field)
     both = multiply(jnp.concatenate([high, low], axis=0), z_high[...])
-    span = planes * rows
-    field = both[:span] + both[span:] + multiply(high, z_low[...])
-    pieces = [field[p * rows : (p + 1) * rows] for p in range(planes)]
-    return [piece[:, :width] for piece in pieces], [piece[:, width:] for piece in pieces]
+    field = both[:rows] + both[rows:] + multiply(high, z_low[...])
+    return field[:, :width], field[:, width:]
 
 
 def total_of(values):
@@ -88,16 +79,16 @@
 
     mine = rows_of(coil)
 
-    def scatter(phase):
+    def scatter(phase, p):
         copies = []
         for distance in range(1, coils):
             target = lax.rem(coil + distance, coils)
             copies.append(
                 pltpu.make_async_remote_copy(
-                    src_ref=part.at[phase, :, :, rows_of(target)],
-                    dst_ref=arrived.at[phase, distance - 1],
-                    send_sem=block_send.at[2 * phase, distance - 1],
-                    recv_sem=block_recv.at[2 * phase, distance - 1],
+                    src_ref=part.at[phase, :, p, rows_of(target)],
+                    dst_ref=arrived.at[phase, distance - 1, :, p],
+                    send_sem=block_send.at[2 * phase, p, distance - 1],
+                    recv_sem=block_recv.at[2 * phase, p, distance - 1],
                     device_id=(slab, target),
                     device_id_type=MESH,
                 )
@@ -106,15 +97,15 @@
             copy.start()
         return copies
 
-    def gather(buffer, phase):
+    def gather(buffer, phase, p):
         copies = []
         for distance in range(1, coils):
             copies.append(
                 pltpu.make_async_remote_copy(
-                    src_ref=buffer.at[:, :, mine],
-                    dst_ref=buffer.at[:, :, mine],
-                    send_sem=block_send.at[2 * phase + 1, distance - 1],
-                    recv_sem=block_recv.at[2 * phase + 1, distance - 1],
+                    src_ref=buffer.at[:, p, mine],
+                    dst_ref=buffer.at[:, p, mine],
+                    send_sem=block_send.at[2 * phase + 1, p, distance - 1],
+                    recv_sem=block_recv.at[2 * phase + 1, p, distance - 1],
                     device_id=(slab, lax.rem(coil + distance, coils)),
                     device_id_type=MESH,
                 )
@@ -158,18 +149,17 @@
             line = line + notes[phase, distance - 1]
         return [jnp.sum(jnp.where(lanes == index, line, 0.0), axis=1, keepdims=True) for index in range(count)]
 
-    def backward_part(real, imag, phase):
+    def backward_part(real, imag, phase, p):
         imag, real = transform(imag, real, *tables)
-        for p in range(planes):
-            part[phase, 0, p] = maps[0, p] * real[p] + maps[1, p] * imag[p]
-            part[phase, 1, p] = maps[0, p] * imag[p] - maps[1, p] * real[p]
-
-    def forward(image):
-        real = [maps[0, p] * image(0, p) - maps[1, p] * image(1, p) for p in range(planes)]
-        imag = [maps[0, p] * image(1, p) + maps[1, p] * image(0, p) for p in range(planes)]
+        part[phase, 0, p] = maps[0, p] * real + maps[1, p] * imag
+        part[phase, 1, p] = maps[0, p] * imag - maps[1, p] * real
+
+    def forward(image_re, image_im, p):
+        real = maps[0, p] * image_re - maps[1, p] * image_im
+        imag = maps[0, p] * image_im + maps[1, p] * image_re
         real, imag = transform(real, imag, *tables)
-        sampled = [mask[p].astype(jnp.float32) for p in range(planes)]
-        return [[real[p] * sampled[p] for p in range(planes)], [imag[p] * sampled[p] for p in range(planes)]]
+        sampled = mask[p].astype(jnp.float32)
+        return real * sampled, imag * sampled
 
     def reduced(phase, h, p):
         value = part[phase, h, p, mine]
@@ -177,57 +167,66 @@
             value = value + arrived[phase, distance - 1, h, p]
         return value
 
-    sampled = [mask[p].astype(jnp.float32) for p in range(planes)]
-    backward_part(
-        [measured[0, p] * sampled[p] for p in range(planes)], [measured[1, p] * sampled[p] for p in range(planes)], 0
-    )
-    finish(scatter(0))
-    entries = [(h, p) for h in range(2) for p in range(planes)]
-    for h, p in entries:
-        rhs[h, p, mine] = reduced(0, h, p) + LAMBDA * prior[h, p]
-    finish(gather(rhs, 0))
-
+    pending = []
+    for p in range(planes):
+        sampled = mask[p].astype(jnp.float32)
+        backward_part(measured[0, p] * sampled, measured[1, p] * sampled, 0, p)
+        pending.append(scatter(0, p))
+    gathers = []
     norm = jnp.zeros((1, 1), jnp.float32)
-    for h, p in entries:
-        value = rhs[h, p, mine]
-        norm = norm + total_of(value * value)
-    result = forward(lambda h, p: rhs[h, p])
+    for p in range(planes):
+        finish(pending[p])
+        for h in range(2):
+            value = reduced(0, h, p) + LAMBDA * prior[h, p]
+            rhs[h, p, mine] = value
+            norm = norm + total_of(value * value)
+        gathers.append(gather(rhs, 0, p))
     energy = LAMBDA * norm
-    for h, p in entries:
-        spectrum[h, p] = result[h][p]
-        energy = energy + total_of(result[h][p] * result[h][p])
-    write_note(0, [norm, energy])
-    first_notes = tell(0)
-    backward_part([spectrum[0, p] for p in range(planes)], [spectrum[1, p] for p in range(planes)], 1)
-    second_parts = scatter(1)
+    pending = []
+    for p in range(planes):
+        finish(gathers[p])
+        result = forward(rhs[0, p], rhs[1, p], p)
+        for h in range(2):
+            spectrum[h, p] = result[h]
+            energy = energy + total_of(result[h] * result[h])
+        if p == planes - 1:
+            write_note(0, [norm, energy])
+            first_notes = tell(0)
+        backward_part(spectrum[0, p], spectrum[1, p], 1, p)
+        pending.append(scatter(1, p))
     finish(first_notes)
     norm, curvature = read_notes(0, 2)
     step = norm / curvature
-    finish(second_parts)
+    gathers = []
     norm_next = jnp.zeros((1, 1), jnp.float32)
     cross = jnp.zeros((1, 1), jnp.float32)
-    for h, p in entries:
-        direction = rhs[h, p, mine]
-        value = direction - step * (reduced(1, h, p) + LAMBDA * direction)
-        own_residual[h, p] = value
-        residual[h, p, mine] = value.astype(jnp.bfloat16)
-        norm_next = norm_next + total_of(value * value)
-        cross = cross + LAMBDA * total_of(value * direction)
-    finish(gather(residual, 1))
-    result = forward(lambda h, p: residual[h, p].astype(jnp.float32))
+    for p in range(planes):
+        finish(pending[p])
+        for h in range(2):
+            direction = rhs[h, p, mine]
+            value = direction - step * (reduced(1, h, p) + LAMBDA * direction)
+            own_residual[h, p] = value
+            residual[h, p, mine] = value.astype(jnp.bfloat16)
+            norm_next = norm_next + total_of(value * value)
+            cross = cross + LAMBDA * total_of(value * direction)
+        gathers.append(gather(residual, 1, p))
     energy = LAMBDA * norm_next
-    for h, p in entries:
-        energy = energy + total_of(result[h][p] * result[h][p])
-        cross = cross + total_of(result[h][p] * spectrum[h, p])
+    for p in range(planes):
+        finish(gathers[p])
+        result = forward(residual[0, p].astype(jnp.float32), residual[1, p].astype(jnp.float32), p)
+        for h in range(2):
+            energy = energy + total_of(result[h] * result[h])
+            cross = cross + total_of(result[h] * spectrum[h, p])
     write_note(1, [norm_next, energy, cross])
     finish(tell(1))
     norm_next, energy, cross = read_notes(1, 3)
     ratio = norm_next / norm
     curvature = energy + 2.0 * ratio * cross + ratio * ratio * curvature
     step_next = norm_next / curvature
-    for h, p in entries:
-        direction = rhs[h, p, mine]
-        out[h, p] = step * direction + step_next * (own_residual[h, p] + ratio * direction)
+    for h in range(2):
+        for p in range(planes):
+            direction = rhs[h, p, mine]
+            out[h, p] = step * direction + step_next * (own_residual[h, p] + ratio * direction)
 
 
 def gradients(maps, measured, mask, prior):
@@ -236,7 +235,7 @@
     shares = lax.axis_size("slab")
     coils = lax.axis_size("coil")
     cosine, sine = dft_parts(rows)
-    y_tables = halves(np.block([[cosine, sine], [-sine, cosine]]))
+    y_tables = halves(np.concatenate([cosine, sine]))
     cosine, sine = dft_parts(width)
     z_tables = halves(np.block([[cosine, -sine], [sine, cosine]]))
     image = (2, planes, rows, width)
@@ -255,8 +254,8 @@
             pltpu.VMEM(image, jnp.bfloat16),
             pltpu.VMEM((2, 1, 128), jnp.float32),
             pltpu.VMEM((2, shares * coils - 1, 1, 128), jnp.float32),
-            pltpu.SemaphoreType.DMA((4, coils - 1)),
-            pltpu.SemaphoreType.DMA((4, coils - 1)),
+            pltpu.SemaphoreType.DMA((4, planes, coils - 1)),
+            pltpu.SemaphoreType.DMA((4, planes, coils - 1)),
             pltpu.SemaphoreType.DMA((2, shares * coils - 1)),
             pltpu.SemaphoreType.DMA((2, shares * coils - 1)),
         ],
@@ -333,7 +332,27 @@
     lax.fori_loop(0, rows // y_outs, step, 0)
 
 
-def denoise_kernel(x_outs, y_outs, group, rows, block_rows, height, features, first, middle, final, out, even, odd):
+def spread_weights(taps, wide, x_outs, y_outs):
+    count, channels = taps.shape[2:]
+    span = (x_outs + 2) * channels
+    empty = jnp.zeros((count, channels), taps.dtype)
+    for x_out in range(x_outs):
+        for y_out in range(y_outs):
+            base = (x_out * y_outs + y_out) * count
+            for y_in in range(y_outs + 2):
+                tap = y_in - y_out
+                if 0 <= tap < 3:
+                    shifts = [x_in - x_out for x_in in range(x_outs + 2)]
+                    pieces = [taps[u, tap] if 0 <= u < 3 else empty for u in shifts]
+                    block = jnp.concatenate(pieces, axis=1)
+                else:
+                    block = jnp.zeros((count, span), taps.dtype)
+                wide[base : base + count, y_in * span : (y_in + 1) * span] = block
+
+
+def denoise_kernel(
+    x_outs, y_outs, group, rows, block_rows, height, features, first, middle, final, out, even, odd, wide
+):
     planes = features.shape[1] - 2
     layers = middle.shape[0] + 2
     top = lax.axis_index("coil") * block_rows + lax.axis_index("slab") * rows
@@ -344,11 +363,13 @@
         buffer[:, planes + 1] = edge
     shared = (planes, x_outs, y_outs, group)
     left = layers - 1
+    for layer in range(layers - 2):
+        spread_weights(middle.at[layer], wide.at[layer], x_outs, y_outs)
     conv_rows(first, features, even, rows + 2 * left, *shared, top - left, height, False)
     for layer in range(layers - 2):
         left = left - 1
         conv_rows(
-            middle.at[layer], buffers[layer % 2], buffers[(layer + 1) % 2],
+            wide.at[layer], buffers[layer % 2], buffers[(layer + 1) % 2],
             rows + 2 * left, *shared, top - left, height, False,
         )
     conv_rows(final, buffers[(layers - 2) % 2], out, rows, *shared, top, height, True)
@@ -365,7 +386,8 @@
     in_rows = 16
     features = jnp.pad(features, ((0, 0), (1, 1), (0, in_rows - features.shape[2]), (0, 0)))
     first = block_weights(w_first, x_outs, y_outs, in_rows - w_first.shape[1], 0)
-    middle = jnp.stack([block_weights(w_middle[m], x_outs, y_outs, 0, 0) for m in range(layers - 2)])
+    middle = jnp.transpose(w_middle, (0, 3, 4, 5, 1, 2)).reshape(layers - 2, 3, 3, 3 * channels, channels)
+    wide = (layers - 2, x_outs * y_outs * 3 * channels, (x_outs + 2) * (y_outs + 2) * channels)
     final = block_weights(w_last, x_outs, y_outs, 0, -w_last.shape[0] % 8)
     outs = w_last.shape[0]
     held = (rows + 2 * (layers - 1), planes + 2, channels, width)
@@ -374,7 +396,7 @@
         out_shape=jax.ShapeDtypeStruct((rows, planes, outs + -outs % 8, width), jnp.float32),
         in_specs=[pl.BlockSpec(memory_space=pltpu.VMEM)] * 4,
         out_specs=pl.BlockSpec(memory_space=pltpu.VMEM),
-        scratch_shapes=[pltpu.VMEM(held, jnp.bfloat16), pltpu.VMEM(held, jnp.bfloat16)],
+        scratch_shapes=[pltpu.VMEM(dims, jnp.bfloat16) for dims in (held, held, wide)],
         compiler_params=pltpu.CompilerParams(vmem_limit_bytes=48 * 1024 * 1024),
     )(features, first, middle, final)
     return result[:, :, :outs]

time: 132 us -> 107 us (0.81)
  local copies, waits for them, and re-layouts: 22.4 us -> 3.95 us
  Pallas kernels: 83.4 us -> 76.8 us
  other arithmetic: 4.18 us -> 1.94 us
  waiting for transfers between devices: 5.52 us -> 7.43 us
    another operation x3 -> x0, local copies, waits for them, and re-layouts: 10.6 us -> none  [denoise(): jnp.stack([block_weights(w_middle[m], x_outs, y_outs, 0, 0) for m in rang...]
    pallas_call x1, Pallas kernels: 65.3 us -> 58.1 us  [gradients(): pl.pallas_call(functools.partial(gradients_kernel, shares, coils), out_sh...]
    another operation x9 -> x4, local copies, waits for them, and re-layouts: 7.72 us -> 0.87 us  [block_weights(): stacked = jnp.stack(parts)]
    ppermute x1, waiting for transfers between devices: 0.01 us -> 3.33 us  [row_halo(): lax.ppermute(head, 'coil', [(i + 1, i) for i in range(count - 1)])]
    another operation x5 -> x2, other arithmetic: 2.43 us -> 0.32 us  [block_weights(): stacked = jnp.stack(parts)]
    all_to_all x1, waiting for transfers between devices: 5.51 us -> 4.1 us  [body(): taken = lax.all_to_all(pieces, 'slab', 0, 0)]
  transfers between devices with their start and end apart: 3 -> 3, of which waited for: 1 -> 2; matrix products, arithmetic and copies ran while one was open for 17% -> 2% of each run, Pallas kernels for 0% -> 0%
where the time goes in v1:
time: 107 us; the launch traced here: 106 us
  Pallas kernels  76.8 us (72%)
  blocking collectives  7.89 us (7%)
  starting transfers between devices  7.46 us (7%)
  waiting for transfers between devices  7.43 us (7%)
  local copies, waits for them, and re-layouts  3.95 us (4%)
  other arithmetic  1.94 us (2%)
    pallas_call x1, Pallas kernels, gradients(): pl.pallas_call(functools.partial(gradients_kernel, shares, coils), out_sh...  58.1 us
    pallas_call x1, Pallas kernels, denoise(): pl.pallas_call(functools.partial(denoise_kernel, x_outs, y_outs, group, r...  18.7 us
    all_to_all x1, blocking collectives, body(): taken = lax.all_to_all(pieces, 'slab', 0, 0)  7.89 us
    all_to_all x1, waiting for transfers between devices, body(): taken = lax.all_to_all(pieces, 'slab', 0, 0)  4.1 us
    all_to_all x1, starting transfers between devices, body(): taken = lax.all_to_all(pieces, 'slab', 0, 0)  3.43 us
    ppermute x1, waiting for transfers between devices, row_halo(): lax.ppermute(head, 'coil', [(i + 1, i) for i in range(count - 1)])  3.33 us
    ppermute x1, starting transfers between devices, row_halo(): lax.ppermute(tail, 'coil', [(i, i + 1) for i in range(count - 1)])  2.73 us
  transfers between devices with their start and end apart: 3, of which 2 were waited for; matrix products, arithmetic and copies ran while one was open for 2% of the time, Pallas kernels for 0%

profile of v1, /device:TPU:0, one launch (start us, length us, event | category | flops | bytes accessed | tf_op | source)
XLA Modules:
  0.0 106.3 jit_solution(18001278770949425894)
XLA Ops:
  0.6 0.0 copy-start.2
  0.6 0.0 copy-start.3
  0.7 58.1 %shard_map.122 = f32[2,2,64,128]{3,2,1,0:T(8,128)} custom-call(f32[2,2,256,128]{3,2,1,0:T(8,128)} %bitcast.76, f32[2,2,256,128]{3,2,1,0:T(8,128)} %bitcast.77, s32[2,256,128]{2,1,0:T(8,128)} %mask.1, f32[2,2,64,128]{3,2,1,0:T(8,128)} %prior.1, bf16[512,256]{1,0:T(8,128)(2,1)} %constant.11.clone.y_high, bf16[512,256]{1,0:T(8,128)(2,1)} %constant.12.clone.y_low, ...), custom_call_target="tpu_custom_call" | custom-call | tf_op jit(solution)/shard_map/pallas_call | solution.py:243
  58.8 0.9 convert_element_type.25
  59.7 2.7 %collective-permute-start = (bf16[2,2,5,128]{3,2,1,0:T(8,128)(2,1)S(1)}, bf16[2,2,5,128]{3,2,1,0:T(8,128)(2,1)S(1)}, u32[]{:S(2)}, u32[]{:S(2)}) collective-permute-start(bf16[2,2,5,128]{3,2,1,0:T(8,128)(2,1)S(1)} %get-tuple-element.6), channel_id=1, source_target_pairs={{0,1},{1,2},{2,3},{4,5},{5,6},{6,7},{8,9},{9,10},{10,11},{12,13},{... | collective-permute-start | bytes 15368 | tf_op jit(solution)/shard_map/ppermute | solution.py:274
  62.4 1.3 %collective-permute-start.1 = (bf16[2,2,5,128]{3,2,1,0:T(8,128)(2,1)S(1)}, bf16[2,2,5,128]{3,2,1,0:T(8,128)(2,1)S(1)}, u32[]{:S(2)}, u32[]{:S(2)}) collective-permute-start(bf16[2,2,5,128]{3,2,1,0:T(8,128)(2,1)S(1)} %get-tuple-element.7), channel_id=1, source_target_pairs={{1,0},{2,1},{3,2},{5,4},{6,5},{7,6},{9,8},{10,9},{11,10},{13,12},{... | collective-permute-start | bytes 15368 | tf_op jit(solution)/shard_map/ppermute | solution.py:276
  63.7 0.0 copy-done.2
  63.8 0.0 copy-done.3
  63.8 0.1 pad_bitcast_fusion.8
  63.9 0.1 pad_bitcast_fusion.3
  64.0 0.1 pad_maximum_fusion.1
  64.1 0.2 copy.25
  64.3 0.3 reshape.25.final
  64.6 0.0 collective-permute-done
  64.7 3.3 %collective-permute-done.1 = bf16[2,2,5,128]{3,2,1,0:T(8,128)(2,1)S(1)} collective-permute-done((bf16[2,2,5,128]{3,2,1,0:T(8,128)(2,1)S(1)}, bf16[2,2,5,128]{3,2,1,0:T(8,128)(2,1)S(1)}, u32[]{:S(2)}, u32[]{:S(2)}) %collective-permute-start.1) | collective-permute-done | bytes 5152 | tf_op jit(solution)/shard_map/ppermute | solution.py:276
  68.1 0.8 copy.22
  68.9 3.4 %all-to-all-start = ((bf16[8,18,2,2,128]{4,3,2,1,0:T(2,128)(2,1)}), bf16[8,18,2,2,128]{4,3,2,1,0:T(2,128)(2,1)S(1)}, u32[]{:S(2)}, u32[]{:S(2)}) async-start(bf16[8,18,2,2,128]{4,3,2,1,0:T(2,128)(2,1)} %copy.22), calls=%async_computation | async-start | bytes 294912 | tf_op jit(solution)/shard_map/all_to_all | solution.py:415
  72.3 0.2 pad_maximum_fusion
  72.5 0.5 copy.24
  73.0 0.7 reshape.23
  73.7 0.0 copy-start
  73.8 0.1 copy.26.first
  73.9 4.1 %all-to-all-done = bf16[8,18,2,2,128]{4,3,2,1,0:T(2,128)(2,1)S(1)} async-done(((bf16[8,18,2,2,128]{4,3,2,1,0:T(2,128)(2,1)}), bf16[8,18,2,2,128]{4,3,2,1,0:T(2,128)(2,1)S(1)}, u32[]{:S(2)}, u32[]{:S(2)}) %all-to-all-start) | async-done | bytes 147488 | tf_op jit(solution)/shard_map/all_to_all | solution.py:415
  78.0 0.1 copy.23
  78.1 0.2 pad.44.features
  78.3 0.0 copy-done
  78.3 0.0 copy-start.1
  78.3 18.7 %shard_map.123 = f32[8,16,8,128]{3,2,1,0:T(8,128)S(1)} custom-call(bf16[18,18,16,128]{3,2,1,0:T(8,128)(2,1)S(1)} %pad.44.features, bf16[384,256]{1,0:T(8,128)(2,1)S(1)} %copy.26.first, bf16[3,3,3,96,32]{4,3,2,1,0:T(8,128)(2,1)S(1)} %bitcast.71, bf16[96,512]{1,0:T(8,128)(2,1)S(1)} %reshape.25.final), custom_call_target="tpu_custom_call" | custom-call | tf_op jit(solution)/shard_map/pallas_call | solution.py:394
  97.1 7.9 %all_to_all.10 = f32[8,8,2,2,128]{4,3,2,1,0:T(2,128)S(1)} all-to-all(f32[8,8,2,2,128]{4,3,2,1,0:T(2,128)S(1)} %bitcast.75), channel_id=1, replica_groups=mesh['slab'=8,'coil'=4] {'slab'}, dimensions={0} | all-to-all | bytes 262144 | tf_op jit(solution)/shard_map/all_to_all | solution.py:420
  105.0 0.0 copy-done.1
  105.0 0.7 bitcast_add_fusion
  105.7 0.7 copy.40
  (14 shorter events, 0.2 us)
Async XLA Ops:
  0.6 63.1 %copy-start.2 = (bf16[2,32,3,3,3]{1,0,4,3,2:T(2,128)(2,1)S(1)}, bf16[2,32,3,3,3]{1,0,4,3,2:T(2,128)(2,1)}, u32[]{:S(2)}) copy-start(bf16[2,32,3,3,3]{1,0,4,3,2:T(2,128)(2,1)} %param.17) | copy-start | bytes 10372
  0.6 63.1 %copy-start.3 = (bf16[32,2,3,3,3]{0,1,4,3,2:T(2,128)(2,1)S(1)}, bf16[32,2,3,3,3]{0,1,4,3,2:T(2,128)(2,1)}, u32[]{:S(2)}) copy-start(bf16[32,2,3,3,3]{0,1,4,3,2:T(2,128)(2,1)} %param.15) | copy-start | bytes 10372
  59.7 4.9 %collective-permute-start = (bf16[2,2,5,128]{3,2,1,0:T(8,128)(2,1)S(1)}, bf16[2,2,5,128]{3,2,1,0:T(8,128)(2,1)S(1)}, u32[]{:S(2)}, u32[]{:S(2)}) collective-permute-start(bf16[2,2,5,128]{3,2,1,0:T(8,128)(2,1)S(1)} %get-tuple-element.6), channel_id=1, source_target_pairs={{0,1},{1,2},{2,3},{4,5},{5,6},{6,7},{8,9},{9,10},{10,11},{12,13},{... | collective-permute-start | bytes 15368 | tf_op jit(solution)/shard_map/ppermute | solution.py:274
  62.4 5.5 %collective-permute-start.1 = (bf16[2,2,5,128]{3,2,1,0:T(8,128)(2,1)S(1)}, bf16[2,2,5,128]{3,2,1,0:T(8,128)(2,1)S(1)}, u32[]{:S(2)}, u32[]{:S(2)}) collective-permute-start(bf16[2,2,5,128]{3,2,1,0:T(8,128)(2,1)S(1)} %get-tuple-element.7), channel_id=1, source_target_pairs={{1,0},{2,1},{3,2},{5,4},{6,5},{7,6},{9,8},{10,9},{11,10},{13,12},{... | collective-permute-start | bytes 15368 | tf_op jit(solution)/shard_map/ppermute | solution.py:276
  68.9 9.1 %all-to-all-start = ((bf16[8,18,2,2,128]{4,3,2,1,0:T(2,128)(2,1)}), bf16[8,18,2,2,128]{4,3,2,1,0:T(2,128)(2,1)S(1)}, u32[]{:S(2)}, u32[]{:S(2)}) async-start(bf16[8,18,2,2,128]{4,3,2,1,0:T(2,128)(2,1)} %copy.22), calls=%async_computation | async-start | bytes 294912 | tf_op jit(solution)/shard_map/all_to_all | solution.py:415
  73.7 4.6 %copy-start = (bf16[3,32,32,3,3,3]{2,1,5,4,3,0:T(8,128)(2,1)S(1)}, bf16[3,32,32,3,3,3]{2,1,5,4,3,0:T(8,128)(2,1)}, u32[]{:S(2)}) copy-start(bf16[3,32,32,3,3,3]{2,1,5,4,3,0:T(8,128)(2,1)} %param.16) | copy-start | bytes 497668
  78.3 26.7 %copy-start.1 = (f32[2,2,64,128]{3,2,1,0:T(8,128)S(1)}, f32[2,2,64,128]{3,2,1,0:T(8,128)}, u32[]{:S(2)}) copy-start(f32[2,2,64,128]{3,2,1,0:T(8,128)} %shard_map.122) | copy-start | bytes 393220

commit v2 on v1

--- a/solution.py
+++ b/solution.py
@@ -54,8 +54,8 @@
 
 def gradients_kernel(
     shares, coils, maps, measured, mask, prior, y_high, y_low, z_high, z_low,
-    out, part, arrived, rhs, spectrum, own_residual, residual, note, notes,
-    block_send, block_recv, note_send, note_recv,
+    out, beside, part, arrived, rhs, spectrum, own_residual, residual, note, notes, edges,
+    block_send, block_recv, note_send, note_recv, edge_send, edge_recv,
 ):
     slab = lax.axis_index("slab")
     coil = lax.axis_index("coil")
@@ -124,6 +124,27 @@
                     send_sem=note_send.at[phase, distance - 1],
                     recv_sem=note_recv.at[phase, distance - 1],
                     device_id=device_at(distance),
+                    device_id_type=MESH,
+                )
+            )
+        for copy in copies:
+            copy.start()
+        return copies
+
+    margin = edges.shape[3]
+    above = lax.rem(coil + coils - 1, coils)
+    below = lax.rem(coil + 1, coils)
+
+    def send_edges(p):
+        copies = []
+        for side, first, target in ((0, block - margin, below), (1, 0, above)):
+            copies.append(
+                pltpu.make_async_remote_copy(
+                    src_ref=own_residual.at[:, p, first : first + margin],
+                    dst_ref=edges.at[side, :, p],
+                    send_sem=edge_send.at[side, p],
+                    recv_sem=edge_recv.at[side, p],
+                    device_id=(slab, target),
                     device_id_type=MESH,
                 )
             )
@@ -209,7 +230,7 @@
             residual[h, p, mine] = value.astype(jnp.bfloat16)
             norm_next = norm_next + total_of(value * value)
             cross = cross + LAMBDA * total_of(value * direction)
-        gathers.append(gather(residual, 1, p))
+        gathers.append(gather(residual, 1, p) + send_edges(p))
     energy = LAMBDA * norm_next
     for p in range(planes):
         finish(gathers[p])
@@ -227,9 +248,15 @@
         for p in range(planes):
             direction = rhs[h, p, mine]
             out[h, p] = step * direction + step_next * (own_residual[h, p] + ratio * direction)
-
-
-def gradients(maps, measured, mask, prior):
+            for side, start, inside in (
+                (0, above * block + block - margin, coil > 0), (1, below * block, coil < coils - 1)
+            ):
+                direction = rhs[h, p, pl.ds(pl.multiple_of(start, margin), margin)]
+                value = step * direction + step_next * (edges[side, h, p] + ratio * direction)
+                beside[side, h, p] = jnp.where(inside, value, 0.0)
+
+
+def gradients(maps, measured, mask, prior, margin):
     planes, rows, width = mask.shape
     block = prior.shape[2]
     shares = lax.axis_size("slab")
@@ -240,11 +267,12 @@
     z_tables = halves(np.block([[cosine, -sine], [sine, cosine]]))
     image = (2, planes, rows, width)
     brick = (2, planes, block, width)
+    margins = (2, 2, planes, margin, width)
     return pl.pallas_call(
         functools.partial(gradients_kernel, shares, coils),
-        out_shape=jax.ShapeDtypeStruct(brick, jnp.float32),
+        out_shape=[jax.ShapeDtypeStruct(dims, jnp.float32) for dims in (brick, margins)],
         in_specs=[pl.BlockSpec(memory_space=pltpu.VMEM)] * 8,
-        out_specs=pl.BlockSpec(memory_space=pltpu.VMEM),
+        out_specs=[pl.BlockSpec(memory_space=pltpu.VMEM)] * 2,
         scratch_shapes=[
             pltpu.VMEM((2,) + image, jnp.float32),
             pltpu.VMEM((2, coils - 1) + brick, jnp.float32),
@@ -254,29 +282,18 @@
             pltpu.VMEM(image, jnp.bfloat16),
             pltpu.VMEM((2, 1, 128), jnp.float32),
             pltpu.VMEM((2, shares * coils - 1, 1, 128), jnp.float32),
+            pltpu.VMEM(margins, jnp.float32),
             pltpu.SemaphoreType.DMA((4, planes, coils - 1)),
             pltpu.SemaphoreType.DMA((4, planes, coils - 1)),
             pltpu.SemaphoreType.DMA((2, shares * coils - 1)),
             pltpu.SemaphoreType.DMA((2, shares * coils - 1)),
+            pltpu.SemaphoreType.DMA((2, planes)),
+            pltpu.SemaphoreType.DMA((2, planes)),
         ],
         compiler_params=pltpu.CompilerParams(
             collective_id=0, has_side_effects=True, vmem_limit_bytes=56 * 1024 * 1024
         ),
     )(maps, measured, mask, prior, *y_tables, *z_tables)
-
-
-def row_halo(cells, width):
-    count = lax.axis_size("coil")
-    tail = cells[:, :, cells.shape[2] - width :]
-    head = cells[:, :, :width]
-    return jnp.concatenate(
-        [
-            lax.ppermute(tail, "coil", [(i, i + 1) for i in range(count - 1)]),
-            cells,
-            lax.ppermute(head, "coil", [(i + 1, i) for i in range(count - 1)]),
-        ],
-        axis=2,
-    )
 
 
 def block_weights(weight, x_outs, y_outs, in_pad, out_pad):
@@ -403,13 +420,15 @@
 
 
 def body(sensitivity, kspace, sampling, prior_image, w_first, w_middle, w_last):
-    brick = gradients(sensitivity[0], kspace[0], sampling, prior_image)
+    halo = w_middle.shape[0] + 2
+    margin = halo + -halo % 8
+    brick, beside = gradients(sensitivity[0], kspace[0], sampling, prior_image, margin)
     len_y = sampling.shape[1]
     block_rows = prior_image.shape[2]
-    halo = w_middle.shape[0] + 2
     shares = lax.axis_size("slab")
     rows = block_rows // shares
-    mine = row_halo(brick.astype(jnp.bfloat16), halo)
+    mine = jnp.concatenate([beside[0, :, :, margin - halo :], brick, beside[1, :, :, :halo]], axis=2)
+    mine = mine.astype(jnp.bfloat16)
     mine = jnp.transpose(mine, (2, 1, 0, 3))
     pieces = jnp.stack([mine[s * rows : (s + 1) * rows + 2 * halo] for s in range(shares)])
     taken = lax.all_to_all(pieces, "slab", 0, 0)

time: 107 us -> 99.8 us (0.933)
  waiting for transfers between devices: 7.43 us -> 3.19 us
  starting transfers between devices: 7.46 us -> 3.41 us
    ppermute x2 -> x0, starting transfers between devices: 4.03 us -> none  [the longest x1 2.73 us: row_halo(): lax.ppermute(tail, 'coil', [(i, i + 1) for i in range(count - 1)])]
    ppermute x2 -> x0, waiting for transfers between devices: 3.33 us -> none  [the longest x1 3.33 us: row_halo(): lax.ppermute(head, 'coil', [(i + 1, i) for i in range(count - 1)])]
    another operation x0 -> x2, other arithmetic: none -> 1.68 us
  transfers between devices with their start and end apart: 3 -> 1, of which waited for: 2 -> 1; matrix products, arithmetic and copies ran while one was open for 2% -> 2% of each run, Pallas kernels for 0% -> 0%
where the time goes in v2:
time: 99.8 us; the launch traced here: 99.4 us
  Pallas kernels  77.4 us (78%)
  blocking collectives  7.89 us (8%)
  local copies, waits for them, and re-layouts  3.95 us (4%)
  starting transfers between devices  3.41 us (3%)
  waiting for transfers between devices  3.19 us (3%)
  other arithmetic  2.71 us (3%)
    pallas_call x1, Pallas kernels, gradients(): pl.pallas_call(functools.partial(gradients_kernel, shares, coils), out_sh...  58.7 us
    pallas_call x1, Pallas kernels, denoise(): pl.pallas_call(functools.partial(denoise_kernel, x_outs, y_outs, group, r...  18.7 us
    all_to_all x1, blocking collectives, body(): taken = lax.all_to_all(pieces, 'slab', 0, 0)  7.89 us
    all_to_all x1, starting transfers between devices, body(): taken = lax.all_to_all(pieces, 'slab', 0, 0)  3.41 us
    all_to_all x1, waiting for transfers between devices, body(): taken = lax.all_to_all(pieces, 'slab', 0, 0)  3.19 us
  transfers between devices with their start and end apart: 1, of which 1 were waited for; matrix products, arithmetic and copies ran while one was open for 2% of the time, Pallas kernels for 0%

profile of v2, /device:TPU:0, one launch (start us, length us, event | category | flops | bytes accessed | tf_op | source)
XLA Modules:
  0.0 99.4 jit_solution(7626511300547898716)
XLA Ops:
  0.6 0.0 copy-start.2
  0.6 58.7 %shard_map.122 = (f32[2,2,64,128]{3,2,1,0:T(8,128)}, f32[2,2,2,8,128]{4,3,2,1,0:T(8,128)}) custom-call(f32[2,2,256,128]{3,2,1,0:T(8,128)} %bitcast.78, f32[2,2,256,128]{3,2,1,0:T(8,128)} %bitcast.79, s32[2,256,128]{2,1,0:T(8,128)} %mask.1, f32[2,2,64,128]{3,2,1,0:T(8,128)} %prior.1, bf16[512,256]{1,0:T(8,128)(2,1)} %constant.11.clone.y_high, ...), custom_call_target="tpu_custom_call" | custom-call | tf_op jit(solution)/shard_map/pallas_call | solution.py:271
  59.4 0.0 copy-start.3
  59.4 0.8 convert.11
  60.2 0.9 convert.12
  61.2 0.8 copy.22
  62.0 3.4 %all-to-all-start = ((bf16[8,18,2,2,128]{4,3,2,1,0:T(2,128)(2,1)}), bf16[8,18,2,2,128]{4,3,2,1,0:T(2,128)(2,1)S(1)}, u32[]{:S(2)}, u32[]{:S(2)}) async-start(bf16[8,18,2,2,128]{4,3,2,1,0:T(2,128)(2,1)} %copy.22), calls=%async_computation | async-start | bytes 294912 | tf_op jit(solution)/shard_map/all_to_all | solution.py:434
  65.4 0.0 copy-done.2
  65.4 0.0 copy-done.3
  65.5 0.1 pad_bitcast_fusion.8
  65.5 0.1 pad_maximum_fusion.1
  65.7 0.2 copy.25
  65.9 0.3 reshape.25.final
  66.2 0.1 pad_bitcast_fusion.3
  66.3 0.2 pad_maximum_fusion
  66.5 0.5 copy.24
  67.0 0.7 reshape.23
  67.7 0.0 copy-start
  67.7 0.1 copy.26.first
  67.9 3.2 %all-to-all-done = bf16[8,18,2,2,128]{4,3,2,1,0:T(2,128)(2,1)S(1)} async-done(((bf16[8,18,2,2,128]{4,3,2,1,0:T(2,128)(2,1)}), bf16[8,18,2,2,128]{4,3,2,1,0:T(2,128)(2,1)S(1)}, u32[]{:S(2)}, u32[]{:S(2)}) %all-to-all-start) | async-done | bytes 147488 | tf_op jit(solution)/shard_map/all_to_all | solution.py:434
  71.1 0.1 copy.23
  71.2 0.2 pad.44.features
  71.4 0.0 copy-done
  71.4 0.0 copy-start.1
  71.4 18.7 %shard_map.123 = f32[8,16,8,128]{3,2,1,0:T(8,128)S(1)} custom-call(bf16[18,18,16,128]{3,2,1,0:T(8,128)(2,1)S(1)} %pad.44.features, bf16[384,256]{1,0:T(8,128)(2,1)S(1)} %copy.26.first, bf16[3,3,3,96,32]{4,3,2,1,0:T(8,128)(2,1)S(1)} %bitcast.75, bf16[96,512]{1,0:T(8,128)(2,1)S(1)} %reshape.25.final), custom_call_target="tpu_custom_call" | custom-call | tf_op jit(solution)/shard_map/pallas_call | solution.py:411
  90.2 7.9 %all_to_all.10 = f32[8,8,2,2,128]{4,3,2,1,0:T(2,128)S(1)} all-to-all(f32[8,8,2,2,128]{4,3,2,1,0:T(2,128)S(1)} %bitcast.81), channel_id=1, replica_groups=mesh['slab'=8,'coil'=4] {'slab'}, dimensions={0} | all-to-all | bytes 262144 | tf_op jit(solution)/shard_map/all_to_all | solution.py:439
  98.1 0.0 copy-done.1
  98.1 0.7 bitcast_add_fusion
  98.7 0.7 copy.40
  (14 shorter events, 0.2 us)
Async XLA Ops:
  0.6 64.8 %copy-start.2 = (bf16[2,32,3,3,3]{1,0,4,3,2:T(2,128)(2,1)S(1)}, bf16[2,32,3,3,3]{1,0,4,3,2:T(2,128)(2,1)}, u32[]{:S(2)}) copy-start(bf16[2,32,3,3,3]{1,0,4,3,2:T(2,128)(2,1)} %param.17) | copy-start | bytes 10372
  59.4 6.1 %copy-start.3 = (bf16[32,2,3,3,3]{0,1,4,3,2:T(2,128)(2,1)S(1)}, bf16[32,2,3,3,3]{0,1,4,3,2:T(2,128)(2,1)}, u32[]{:S(2)}) copy-start(bf16[32,2,3,3,3]{0,1,4,3,2:T(2,128)(2,1)} %param.15) | copy-start | bytes 10372
  62.0 9.1 %all-to-all-start = ((bf16[8,18,2,2,128]{4,3,2,1,0:T(2,128)(2,1)}), bf16[8,18,2,2,128]{4,3,2,1,0:T(2,128)(2,1)S(1)}, u32[]{:S(2)}, u32[]{:S(2)}) async-start(bf16[8,18,2,2,128]{4,3,2,1,0:T(2,128)(2,1)} %copy.22), calls=%async_computation | async-start | bytes 294912 | tf_op jit(solution)/shard_map/all_to_all | solution.py:434
  67.7 3.7 %copy-start = (bf16[3,32,32,3,3,3]{2,1,5,4,3,0:T(8,128)(2,1)S(1)}, bf16[3,32,32,3,3,3]{2,1,5,4,3,0:T(8,128)(2,1)}, u32[]{:S(2)}) copy-start(bf16[3,32,32,3,3,3]{2,1,5,4,3,0:T(8,128)(2,1)} %param.16) | copy-start | bytes 497668
  71.4 26.7 %copy-start.1 = (f32[2,2,64,128]{3,2,1,0:T(8,128)S(1)}, f32[2,2,64,128]{3,2,1,0:T(8,128)}, u32[]{:S(2)}) copy-start(f32[2,2,64,128]{3,2,1,0:T(8,128)} %get-tuple-element.18) | copy-start | bytes 393220
